TPU v7x, 256 devices: a whole 4x4x8 slice. The times are simulated.
256 devices in a mesh: dp: 32 (over x, z_lo, y), tensor: 8 (over z_hi, core).
Axes of the slice: x: 4, y: 4, z: 8 (z_hi: 4, z_lo: 2; z = z_hi * 2 + z_lo), core: 2. Of those that a mesh axis runs over, the one named last changes fastest.
Arguments:
- gradient: bfloat16 [2, 2048, 16384], P(None, 'dp', 'tensor'), may hold values from -1000 to 1000
- master: float32 [2, 2048, 16384], P(None, 'dp', 'tensor'), may hold values from -0.046875 to 0.046875
- first_moment: float32 [2, 2048, 16384], P(None, 'dp', 'tensor'), may hold values from -3 to 3
- second_moment: float32 [2, 2048, 16384], P(None, 'dp', 'tensor'), may hold values from 0.05 to 1
- residual: bfloat16 [8192, 16384], P('dp', 'tensor'), may hold values from -1500 to 1500
- norm_gain: float32 [16384], replicated, may hold values from 0.5 to 2
- queries: bfloat16 [8192, 128, 128], P('dp', 'tensor'), may hold values from -170 to 170
- layer_cache: bfloat16 [8192, 2, 8, 32, 128], P('dp', None, 'tensor'), may hold values from -4.5 to 4.5
- fresh_entries: bfloat16 [8192, 2, 8, 128], P('dp', None, 'tensor'), may hold values from -6 to 6
- lengths: int32 [8192], P('dp'), may hold values from 2 to 32, as said below
- shard_table: int32 [32], replicated, may hold values from 0 to 31, each once
Outputs:
- new_first: float32 [2, 2048, 16384], P(None, 'dp', 'tensor')
- new_second: float32 [2, 2048, 16384], P(None, 'dp', 'tensor')
- attended: bfloat16 [8192, 128, 128], P('dp', 'tensor')
- activated: bfloat16 [8192, 2048], P('dp', 'tensor')
Inputs may be any that keep to these rules, and one draw needn't show every extreme that they name: `lengths`: every row has 2 or more valid positions, and in each rollout group's rows one row has all 32. `shard_table`: A permutation of the learner shards.
All inputs are finite; a program needn't handle non-finite values.
Results may differ from a plain program's by a relative error of at most 0.0072.
Values may be sent and summed in bfloat16 or wider, within the bound.
A program may use at most 128 MiB of HBM per device.

v0:
```python
import math
import jax
import jax.numpy as jnp
from jax import lax
from jax.sharding import PartitionSpec as P

LEARN_RATE = 0.001
CLIP_LEVEL = 0.5
CLIP_EPSILON = 1e-06
FIRST_DECAY = 0.9
SECOND_DECAY = 0.95
FIRST_CORRECTION = 1.0 - 0.9**10
SECOND_CORRECTION = 1.0 - 0.95**10
ADAM_EPSILON = 1e-08
NORM_EPSILON = 1e-05


def adam_update(gradient, master, first_moment, second_moment):
    entry_count = (
        gradient.shape[0]
        * gradient.shape[1]
        * lax.axis_size("dp")
        * gradient.shape[2]
        * lax.axis_size("tensor")
    )
    gradient_wide = gradient.astype(jnp.float32)
    local_sum = jnp.sum(gradient_wide * gradient_wide)
    total_sum = lax.psum(local_sum, ("dp", "tensor"))
    clip_limit = CLIP_LEVEL * math.sqrt(entry_count)
    clip_factor = jnp.minimum(1.0, clip_limit / (jnp.sqrt(total_sum) + CLIP_EPSILON))
    clipped = gradient_wide * clip_factor
    new_first = FIRST_DECAY * first_moment + (1.0 - FIRST_DECAY) * clipped
    new_second = SECOND_DECAY * second_moment + (1.0 - SECOND_DECAY) * clipped * clipped
    adam_step = (
        new_first / FIRST_CORRECTION / (jnp.sqrt(new_second / SECOND_CORRECTION) + ADAM_EPSILON)
    )
    fresh_weight = (master - LEARN_RATE * adam_step).astype(jnp.bfloat16)
    return (new_first, new_second, fresh_weight)


def attend(queries, layer_cache, fresh_entries, lengths):
    row_count, head_count, head_width = queries.shape
    group_count = layer_cache.shape[2]
    per_group = head_count // group_count
    score_scale = 1.0 / math.sqrt(head_width)
    grouped = queries.reshape(row_count, group_count, per_group, head_width)
    cached_keys = layer_cache[:, 0]
    cached_values = layer_cache[:, 1]
    scores = (
        jnp.einsum("rghd,rgpd->rghp", grouped, cached_keys, preferred_element_type=jnp.float32)
        * score_scale
    )
    own_score = (
        jnp.einsum(
            "rghd,rgd->rgh", grouped, fresh_entries[:, 0], preferred_element_type=jnp.float32
        )
        * score_scale
    )
    positions = lax.broadcasted_iota(jnp.int32, (row_count, 1, 1, cached_keys.shape[2]), 3)
    in_range = positions < lengths[:, None, None, None]
    scores = jnp.where(in_range, scores, -jnp.inf)
    row_peak = jnp.maximum(jnp.max(scores, axis=3), own_score)
    cached_exp = jnp.exp(scores - row_peak[..., None])
    own_exp = jnp.exp(own_score - row_peak)
    denominator = jnp.sum(cached_exp, axis=3) + own_exp
    cached_prob = (cached_exp / denominator[..., None]).astype(jnp.bfloat16)
    own_prob = (own_exp / denominator).astype(jnp.bfloat16)
    combined = jnp.einsum(
        "rghp,rgpd->rghd", cached_prob, cached_values, preferred_element_type=jnp.float32
    )
    combined = (
        combined
        + own_prob[..., None].astype(jnp.float32)
        * fresh_entries[:, 1].astype(jnp.float32)[:, :, None, :]
    )
    return combined.reshape(row_count, head_count, head_width).astype(jnp.bfloat16)


def per_device(
    gradient,
    master,
    first_moment,
    second_moment,
    residual,
    norm_gain,
    queries,
    layer_cache,
    fresh_entries,
    lengths,
    shard_table,
):
    new_first, new_second, fresh_weight = adam_update(gradient, master, first_moment, second_moment)
    row_count = residual.shape[0]
    shard_count = lax.axis_size("dp")
    rank_count = lax.axis_size("tensor")
    unit_block = fresh_weight.shape[1] // rank_count
    gathered = lax.all_gather(residual, "tensor", axis=1, tiled=True)
    gathered_wide = gathered.astype(jnp.float32)
    mean_square = jnp.mean(gathered_wide * gathered_wide, axis=1, keepdims=True)
    normed = (gathered_wide * lax.rsqrt(mean_square + NORM_EPSILON) * norm_gain).astype(
        jnp.bfloat16
    )
    regrouped = lax.all_to_all(fresh_weight, "tensor", split_axis=1, concat_axis=2, tiled=True)
    projected = jnp.einsum(
        "xk,cuk->xcu",
        normed,
        lax.all_gather(regrouped, "dp", axis=1, tiled=True),
        preferred_element_type=jnp.float32,
    )
    projected = projected.reshape(row_count, 2, shard_count, unit_block)
    hidden = jax.nn.silu(projected[:, 0]) * projected[:, 1]
    ordered = jnp.take(hidden, shard_table, axis=1)
    activated = ordered.reshape(row_count, shard_count * unit_block).astype(jnp.bfloat16)
    attended = attend(queries, layer_cache, fresh_entries, lengths)
    return (new_first, new_second, attended, activated)


def solution(mesh):
    return jax.shard_map(
        per_device,
        mesh=mesh,
        in_specs=(
            P(None, "dp", "tensor"),
            P(None, "dp", "tensor"),
            P(None, "dp", "tensor"),
            P(None, "dp", "tensor"),
            P("dp", "tensor"),
            P(),
            P("dp", "tensor", None),
            P("dp", None, "tensor", None, None),
            P("dp", None, "tensor", None),
            P("dp"),
            P(),
        ),
        out_specs=(
            P(None, "dp", "tensor"),
            P(None, "dp", "tensor"),
            P("dp", "tensor", None),
            P("dp", "tensor"),
        ),
        check_vma=False,
    )
```

profile of v0, /device:TPU:64, one launch (start us, length us, event | category | flops | bytes accessed | tf_op | source)
XLA Modules:
  0.0 359.4 jit_solution(8791076577248445641)
XLA Ops:
  7.2 0.0 copy-start
  7.2 0.0 copy-start.1
  7.2 0.0 all-gather.3.cloned.1.call-start
  7.2 0.7 all-gather.3.cloned.1.call-update
  7.9 0.0 all-gather.5.cloned.1.call-start
  8.0 1.9 fusion.23
  9.9 110.7 %psum.7 = f32[]{:T(128)} all-reduce(f32[]{:T(128)} %fusion.23), channel_id=1, replica_groups=mesh['dp'=32,'tensor'=8] {'dp','tensor'}, use_global_device_ids=true, to_apply=%region_1.0 | all-reduce | flops 1 | bytes 8 | tf_op jit(solution)/shard_map/psum | solution.py:28
  121.3 0.0 copy-done.1
  121.3 3.8 %subtract_convert_fusion = (bf16[2,64,2048]{2,1,0:T(8,128)(2,1)S(1)}, f32[2,64,2048]{2,1,0:T(8,128)}, f32[2,64,2048]{2,1,0:T(8,128)}) fusion(f32[2,64,2048]{2,1,0:T(8,128)S(1)} %copy-done.1, f32[]{:T(128)S(6)} %min_shard_map.3, bf16[2,64,2048]{2,1,0:T(8,128)(2,1)} %param.11, f32[2,64,2048]{2,1,0:T(8,128)} %param.14, f32[2,64,2048]{2,1,0:T(8,128)} %param.13), kind=kLoop, calls=%fused_computation.30 | loop fusion | flops 4194304 | bytes 6291460 | tf_op jit(solution)/shard_map/convert_element_type | solution.py:37
  125.1 0.5 copy.36
  125.7 21.1 %all_to_all.18 = bf16[2,64,2048]{2,0,1:T(2,128)(2,1)S(1)} all-to-all(bf16[2,64,2048]{2,0,1:T(2,128)(2,1)S(1)} %copy.36), channel_id=1, replica_groups=mesh['dp'=32,'tensor'=8] {'tensor'}, dimensions={1} | all-to-all | bytes 1048576 | tf_op jit(solution)/shard_map/all_to_all | solution.py:103
  146.8 1.0 copy.37
  147.8 0.0 all-gather.5.cloned.1.call-update
  147.8 0.0 copy-done.3
  147.9 0.2 fusion.40
  148.1 0.1 broadcast_in_dim.37
  148.2 0.1 broadcast_in_dim.38
  148.3 0.0 copy-done.4
  148.3 0.1 iota_compare_fusion
  148.4 0.7 fusion.32
  149.1 3.1 fusion.14
  152.2 1.3 fusion.15
  153.5 0.1 fusion.35
  153.6 0.0 copy-done.2
  153.6 3.7 %add_convert_fusion = bf16[256,16,128]{2,1,0:T(8,128)(2,1)} fusion(bf16[256,2,1,32,128]{4,3,2,1,0:T(8,128)(2,1)S(1)} %copy-done.2, f32[256,16,32]{2,1,0:T(8,128)S(1)} %get-tuple-element.24, f32[256,128]{1,0:T(8,128)S(1)} %bitcast.54, f32[256,16]{1,0:T(8,128)S(1)} %get-tuple-element.20, f32[256,16]{1,0:T(8,128)S(1)} %get-tuple-element.19, ...), kind=kOutput, calls=%fused_computation.14 | convolution fusion | flops 35782656 | bytes 5799936 | tf_op jit(solution)/shard_map/rghp,rgpd->rghd/dot_general | solution.py:68
  157.3 5.2 %fusion = f32[256]{0:T(256)S(1)} fusion(bf16[256,16384]{1,0:T(8,128)(2,1)} %all-gather.3.cloned.1.call-done), kind=kLoop, calls=%fused_computation.3 | loop fusion | flops 12582656 | bytes 8389632 | tf_op jit(solution)/shard_map/reduce_sum | solution.py:99
  162.5 176.5 %all-gather.5.cloned.1.call-done = bf16[2,256,16384]{2,1,0:T(8,128)(2,1)} async-done(((bf16[2,8,16384]{2,1,0:T(8,128)(2,1)}), bf16[2,256,16384]{2,1,0:T(8,128)(2,1)}) %all-gather.5.cloned.1.call-update) | async-done | bytes 16777232 | tf_op jit(solution)/shard_map/all_gather | solution.py:107
  339.0 12.0 %fusion.19 = f32[256,2,32,8]{0,3,2,1:T(8,128)S(1)} fusion(bf16[2,256,16384]{2,1,0:T(8,128)(2,1)} %all-gather.5.cloned.1.call-done, bf16[256,16384]{1,0:T(8,128)(2,1)} %all-gather.3.cloned.1.call-done, f32[16384]{0:T(1024)S(1)} %copy-done.5, f32[256]{0:T(256)S(1)} %add_rsqrt_fusion), kind=kOutput, calls=%fused_computation.26 | convolution fusion | flops 4311744512 | bytes 25756672 | tf_op jit(solution)/shard_map/xk,cuk->xcu/dot_general | solution.py:104
  351.0 0.1 fusion.30
  351.1 0.6 gather_fusion
  351.7 0.1 fusion.31
  351.8 0.8 copy.38
  (15 shorter events, 0.1 us)
Async XLA Ops:
  7.2 141.2 %copy-start = (bf16[256,16,128]{2,1,0:T(8,128)(2,1)S(1)}, bf16[256,16,128]{2,1,0:T(8,128)(2,1)}, u32[]{:S(2)}) copy-start(bf16[256,16,128]{2,1,0:T(8,128)(2,1)} %param.17) | copy-start | bytes 3145732
  7.2 114.1 %copy-start.1 = (f32[2,64,2048]{2,1,0:T(8,128)S(1)}, f32[2,64,2048]{2,1,0:T(8,128)}, u32[]{:S(2)}) copy-start(f32[2,64,2048]{2,1,0:T(8,128)} %param.12) | copy-start | bytes 3145732
  7.2 150.1 %all-gather.3.cloned.1.call-start = ((), (), s32[]{:S(2)}) async-start(), calls=%async_computation.1 | async-start | bytes 9437184 | tf_op jit(solution)/shard_map/all_gather | solution.py:97
  7.9 331.0 %all-gather.5.cloned.1.call-start = ((), (), s32[]{:S(2)}) async-start(), calls=%async_computation.2 | async-start | bytes 17301504 | tf_op jit(solution)/shard_map/all_gather | solution.py:107
  125.1 22.7 %copy-start.3 = (bf16[256,2,1,128]{3,1,2,0:T(2,128)(2,1)S(1)}, bf16[256,2,1,128]{3,1,2,0:T(2,128)(2,1)}, u32[]{:S(2)}) copy-start(bf16[256,2,1,128]{3,1,2,0:T(2,128)(2,1)} %param.19) | copy-start | bytes 393220
  125.1 22.9 %copy-start.6 = (s32[32]{0:T(128)S(1)}, s32[32]{0:T(128)}, u32[]{:S(2)}) copy-start(s32[32]{0:T(128)} %param.21) | copy-start | bytes 388
  125.1 23.2 %copy-start.4 = (s32[256]{0:T(256)S(1)}, s32[256]{0:T(256)}, u32[]{:S(2)}) copy-start(s32[256]{0:T(256)} %param.20) | copy-start | bytes 3076
  149.1 4.5 %copy-start.2 = (bf16[256,2,1,32,128]{4,3,2,1,0:T(8,128)(2,1)S(1)}, bf16[256,2,1,32,128]{4,3,2,1,0:T(8,128)(2,1)}, u32[]{:S(2)}) copy-start(bf16[256,2,1,32,128]{4,3,2,1,0:T(8,128)(2,1)} %param.18) | copy-start | bytes 12582916
  157.3 181.7 %copy-start.5 = (f32[16384]{0:T(1024)S(1)}, f32[16384]{0:T(1024)}, u32[]{:S(2)}) copy-start(f32[16384]{0:T(1024)} %param.16) | copy-start | bytes 196612
Sparse Core Ops, SparseCore 0:
  9.9 90.7 all-gather.2
  148.0 190.9 all-gather.4
where the time goes:
time: 360 us; the launch traced here: 359 us
  waiting for transfers between devices  177 us (49%)
  blocking collectives  132 us (37%)
  matrix products  19.5 us (5%)
  between operations  15 us (4%)
  other arithmetic  12.8 us (4%)
    all_gather x1, waiting for transfers between devices, per_device(): lax.all_gather(regrouped, 'dp', axis=1, tiled=True)  177 us
    psum x1, blocking collectives, adam_update(): total_sum = lax.psum(local_sum, ('dp', 'tensor'))  111 us
    all_to_all x1, blocking collectives, per_device(): lax.all_to_all(fresh_weight, 'tensor', split_axis=1, concat_axis=2, tiled...  21.1 us
    dot_general x1, matrix products, per_device(): jnp.einsum('xk,cuk->xcu', normed, lax.all_gather(regrouped, 'dp', axis=1,...  12 us
  transfers between devices with their start and end apart: 2, of which 1 were waited for; matrix products, arithmetic and copies ran while one was open for 6% of the time, Pallas kernels for 0%

commit v1 on v0

--- a/solution.py
+++ b/solution.py
@@ -104,7 +104,9 @@
     projected = jnp.einsum(
         "xk,cuk->xcu",
         normed,
-        lax.all_gather(regrouped, "dp", axis=1, tiled=True),
+        jnp.concatenate(
+            lax.all_to_all(jnp.stack([regrouped] * lax.axis_size("dp")), "dp", 0, 0), axis=1
+        ),
         preferred_element_type=jnp.float32,
     )
     projected = projected.reshape(row_count, 2, shard_count, unit_block)

time: 360 us -> 484 us (1.34)
  the two profiles are of different devices: /device:TPU:64 before, /device:TPU:2 now
where the time goes in v1:
time: 484 us
  waiting for transfers between devices  311 us (64%)
  blocking collectives  101 us (21%)
  matrix products  27.9 us (6%)
  between operations  15 us (3%)
  other arithmetic  13.3 us (3%)
  local copies, waits for them, and re-layouts  8.7 us (2%)
  starting transfers between devices  7.48 us (2%)
    all_to_all x1, waiting for transfers between devices, per_device(): lax.all_to_all(jnp.stack([regrouped] * lax.axis_size('dp')), 'dp', 0, 0)  198 us
    all_gather x1, waiting for transfers between devices, per_device(): gathered = lax.all_gather(residual, 'tensor', axis=1, tiled=True)  113 us
    psum x1, blocking collectives, adam_update(): total_sum = lax.psum(local_sum, ('dp', 'tensor'))  78.6 us
    all_to_all x1, blocking collectives, per_device(): lax.all_to_all(fresh_weight, 'tensor', split_axis=1, concat_axis=2, tiled...  22 us
    dot_general x1, matrix products, per_device(): jnp.einsum('xk,cuk->xcu', normed, jnp.concatenate(lax.all_to_all(jnp.stac...  20.5 us
  transfers between devices with their start and end apart: 2, of which 2 were waited for; matrix products, arithmetic and copies ran while one was open for 3% of the time, Pallas kernels for 0%

profile of v1, /device:TPU:2, one launch (start us, length us, event | category | flops | bytes accessed | tf_op | source)
XLA Modules:
  0.0 484.0 jit_solution(8664016577002714842)
XLA Ops:
  7.2 0.0 copy-start
  7.2 2.0 fusion.22
  9.2 78.6 %psum.7 = f32[]{:T(128)} all-reduce(f32[]{:T(128)} %fusion.22), channel_id=1, replica_groups=mesh['dp'=32,'tensor'=8] {'dp','tensor'}, use_global_device_ids=true, to_apply=%region_1.0 | all-reduce | flops 1 | bytes 8 | tf_op jit(solution)/shard_map/psum | solution.py:28
  88.5 4.1 subtract_convert_fusion
  92.7 0.5 copy.50
  93.2 22.0 %all_to_all.20 = bf16[2,64,2048]{2,0,1:T(2,128)(2,1)S(1)} all-to-all(bf16[2,64,2048]{2,0,1:T(2,128)(2,1)S(1)} %copy.50), channel_id=1, replica_groups=mesh['dp'=32,'tensor'=8] {'tensor'}, dimensions={1} | all-to-all | bytes 1048576 | tf_op jit(solution)/shard_map/all_to_all | solution.py:103
  115.3 0.3 copy.69
  115.6 0.2 stack.4
  115.8 6.0 %stack.5 = bf16[32,2,8,16384]{3,2,1,0:T(8,128)(2,1)} broadcast(bf16[2,8,16384]{2,1,0:T(8,128)(2,1)S(1)} %stack.4), dimensions={1,2,3} | broadcast | bytes 17301504 | tf_op jit(solution)/shard_map/stack | solution.py:108
  121.8 7.4 %all-to-all-start.1 = ((bf16[32,2,8,16384]{3,2,1,0:T(8,128)(2,1)}), bf16[32,2,8,16384]{3,2,1,0:T(8,128)(2,1)}, u32[]{:S(2)}, u32[]{:S(2)}) async-start(bf16[32,2,8,16384]{3,2,1,0:T(8,128)(2,1)} %stack.5), calls=%async_computation.1 | async-start | bytes 33554432 | tf_op jit(solution)/shard_map/all_to_all | solution.py:108
  129.3 0.0 all-gather.2.cloned.1.call-start
  129.3 0.7 all-gather.2.cloned.1.call-update
  130.0 0.0 copy-done.2
  130.0 0.2 fusion.39
  130.2 0.0 copy-done.5
  130.2 0.1 broadcast_in_dim.37
  130.3 0.1 broadcast_in_dim.38
  130.4 0.1 iota_compare_fusion
  130.6 0.6 fusion.31
  131.2 3.1 fusion.16
  134.3 1.5 fusion.17
  135.8 0.1 fusion.34
  135.9 3.7 add_convert_fusion
  139.6 112.7 %all-gather.2.cloned.1.call-done = bf16[256,16384]{1,0:T(8,128)(2,1)} async-done(((bf16[256,2048]{1,0:T(8,128)(2,1)}), bf16[256,16384]{1,0:T(8,128)(2,1)}) %all-gather.2.cloned.1.call-update) | async-done | bytes 8388624 | tf_op jit(solution)/shard_map/all_gather | solution.py:97
  252.3 5.1 %fusion = f32[256]{0:T(256)S(1)} fusion(bf16[256,16384]{1,0:T(8,128)(2,1)} %all-gather.2.cloned.1.call-done), kind=kLoop, calls=%fused_computation.3 | loop fusion | flops 12582656 | bytes 8389632 | tf_op jit(solution)/shard_map/reduce_sum | solution.py:99
  257.4 197.6 %all-to-all-done.1 = bf16[32,2,8,16384]{3,2,1,0:T(8,128)(2,1)} async-done(((bf16[32,2,8,16384]{3,2,1,0:T(8,128)(2,1)}), bf16[32,2,8,16384]{3,2,1,0:T(8,128)(2,1)}, u32[]{:S(2)}, u32[]{:S(2)}) %all-to-all-start.1) | async-done | bytes 16777248 | tf_op jit(solution)/shard_map/all_to_all | solution.py:108
  455.1 20.5 %fusion.3 = f32[256,2,32,8]{0,2,3,1:T(8,128)S(1)} fusion(bf16[32,2,8,16384]{3,2,1,0:T(8,128)(2,1)} %all-to-all-done.1, bf16[256,16384]{1,0:T(8,128)(2,1)} %all-gather.2.cloned.1.call-done, f32[16384]{0:T(1024)S(1)} %copy-done.4, f32[256]{0:T(256)S(1)} %add_rsqrt_fusion), kind=kOutput, calls=%fused_computation.6 | convolution fusion | flops 4311744512 | bytes 25756672 | tf_op jit(solution)/shard_map/xk,cuk->xcu/dot_general | solution.py:104
  475.5 0.1 fusion.29
  475.6 0.1 copy.53
  475.7 0.6 gather_fusion
  476.3 0.1 fusion.30
  476.4 0.8 copy.54
  (15 shorter events, 0.1 us)
Async XLA Ops:
  7.2 123.4 %copy-start = (bf16[256,16,128]{2,1,0:T(8,128)(2,1)S(1)}, bf16[256,16,128]{2,1,0:T(8,128)(2,1)}, u32[]{:S(2)}) copy-start(bf16[256,16,128]{2,1,0:T(8,128)(2,1)} %param.17) | copy-start | bytes 3145732
  121.8 8.2 %copy-start.2 = (bf16[256,2,1,128]{3,1,2,0:T(2,128)(2,1)S(1)}, bf16[256,2,1,128]{3,1,2,0:T(2,128)(2,1)}, u32[]{:S(2)}) copy-start(bf16[256,2,1,128]{3,1,2,0:T(2,128)(2,1)} %param.19) | copy-start | bytes 393220
  121.8 8.4 %copy-start.5 = (s32[32]{0:T(128)S(1)}, s32[32]{0:T(128)}, u32[]{:S(2)}) copy-start(s32[32]{0:T(128)} %param.21) | copy-start | bytes 388
  121.8 8.6 %copy-start.3 = (s32[256]{0:T(256)S(1)}, s32[256]{0:T(256)}, u32[]{:S(2)}) copy-start(s32[256]{0:T(256)} %param.20) | copy-start | bytes 3076
  121.8 333.2 %all-to-all-start.1 = ((bf16[32,2,8,16384]{3,2,1,0:T(8,128)(2,1)}), bf16[32,2,8,16384]{3,2,1,0:T(8,128)(2,1)}, u32[]{:S(2)}, u32[]{:S(2)}) async-start(bf16[32,2,8,16384]{3,2,1,0:T(8,128)(2,1)} %stack.5), calls=%async_computation.1 | async-start | bytes 33554432 | tf_op jit(solution)/shard_map/all_to_all | solution.py:108
  129.3 123.0 %all-gather.2.cloned.1.call-start = ((), (), s32[]{:S(2)}) async-start(), calls=%async_computation.2 | async-start | bytes 9437184 | tf_op jit(solution)/shard_map/all_gather | solution.py:97
  131.2 4.7 copy-start.1
  139.6 315.5 %copy-start.4 = (f32[16384]{0:T(1024)S(1)}, f32[16384]{0:T(1024)}, u32[]{:S(2)}) copy-start(f32[16384]{0:T(1024)} %param.16) | copy-start | bytes 196612
Sparse Core Ops, SparseCore 0:
  131.9 120.2 all-gather.1

commit v2 on v0

--- a/solution.py
+++ b/solution.py
@@ -100,7 +100,12 @@
     normed = (gathered_wide * lax.rsqrt(mean_square + NORM_EPSILON) * norm_gain).astype(
         jnp.bfloat16
     )
-    regrouped = lax.all_to_all(fresh_weight, "tensor", split_axis=1, concat_axis=2, tiled=True)
+    regrouped = jnp.concatenate(
+        lax.all_to_all(
+            jnp.stack(jnp.split(fresh_weight, lax.axis_size("tensor"), axis=1)), "tensor", 0, 0
+        ),
+        axis=2,
+    )
     projected = jnp.einsum(
         "xk,cuk->xcu",
         normed,

time: 360 us -> 359 us (level)
  no operation moved by 1% of the time
where the time goes in v2:
time: 359 us
  waiting for transfers between devices  177 us (49%)
  blocking collectives  132 us (37%)
  matrix products  19.5 us (5%)
  between operations  15 us (4%)
  other arithmetic  12.8 us (4%)
    all_gather x1, waiting for transfers between devices, per_device(): lax.all_gather(regrouped, 'dp', axis=1, tiled=True)  177 us
    psum x1, blocking collectives, adam_update(): total_sum = lax.psum(local_sum, ('dp', 'tensor'))  111 us
    all_to_all x1, blocking collectives, per_device(): lax.all_to_all(jnp.stack(jnp.split(fresh_weight, lax.axis_size('tensor'),...  21.1 us
    dot_general x1, matrix products, per_device(): jnp.einsum('xk,cuk->xcu', normed, lax.all_gather(regrouped, 'dp', axis=1,...  12 us
  transfers between devices with their start and end apart: 2, of which 1 were waited for; matrix products, arithmetic and copies ran while one was open for 6% of the time, Pallas kernels for 0%

profile of v2, /device:TPU:64, one launch (start us, length us, event | category | flops | bytes accessed | tf_op | source)
XLA Modules:
  0.0 358.8 jit_solution(10007632531197399855)
XLA Ops:
  7.2 0.0 copy-start
  7.2 0.0 copy-start.1
  7.2 0.0 all-gather.3.cloned.1.call-start
  7.2 0.7 all-gather.3.cloned.1.call-update
  7.9 0.0 all-gather.5.cloned.1.call-start
  8.0 1.9 fusion.23
  9.9 110.7 %psum.7 = f32[]{:T(128)} all-reduce(f32[]{:T(128)} %fusion.23), channel_id=1, replica_groups=mesh['dp'=32,'tensor'=8] {'dp','tensor'}, use_global_device_ids=true, to_apply=%region_1.0 | all-reduce | flops 1 | bytes 8 | tf_op jit(solution)/shard_map/psum | solution.py:28
  121.3 0.0 copy-done.1
  121.3 3.8 %subtract_convert_fusion = (bf16[2,64,2048]{2,1,0:T(8,128)(2,1)S(1)}, f32[2,64,2048]{2,1,0:T(8,128)}, f32[2,64,2048]{2,1,0:T(8,128)}) fusion(f32[2,64,2048]{2,1,0:T(8,128)S(1)} %copy-done.1, f32[]{:T(128)S(6)} %min_shard_map.3, bf16[2,64,2048]{2,1,0:T(8,128)(2,1)} %param.11, f32[2,64,2048]{2,1,0:T(8,128)} %param.14, f32[2,64,2048]{2,1,0:T(8,128)} %param.13), kind=kLoop, calls=%fused_computation.30 | loop fusion | flops 4194304 | bytes 6291460 | tf_op jit(solution)/shard_map/convert_element_type | solution.py:37
  125.2 0.0 copy-start.4
  125.3 21.1 %all_to_all.5 = bf16[8,2,8,2048]{3,2,1,0:T(8,128)(2,1)S(1)} all-to-all(bf16[8,2,8,2048]{3,2,1,0:T(8,128)(2,1)S(1)} %fusion.35), channel_id=1, replica_groups=mesh['dp'=32,'tensor'=8] {'tensor'}, dimensions={0} | all-to-all | bytes 1048576 | tf_op jit(solution)/shard_map/all_to_all | solution.py:104
  146.4 0.9 copy.22
  147.3 0.0 all-gather.5.cloned.1.call-update
  147.3 0.0 copy-done.6
  147.3 0.1 broadcast_in_dim.37
  147.4 0.1 broadcast_in_dim.38
  147.5 0.0 copy-done.3
  147.5 0.2 fusion.48
  147.7 0.0 copy-done.4
  147.8 0.1 iota_compare_fusion
  147.9 0.7 fusion.32
  148.5 3.1 fusion.14
  151.6 1.3 fusion.15
  152.9 0.1 fusion.43
  153.0 3.7 %add_convert_fusion = bf16[256,16,128]{2,1,0:T(8,128)(2,1)} fusion(bf16[256,2,1,32,128]{4,3,2,1,0:T(8,128)(2,1)S(1)} %copy-done.2, f32[256,16,32]{2,1,0:T(8,128)S(1)} %get-tuple-element.16, f32[256,128]{1,0:T(8,128)S(1)} %bitcast.84, f32[256,16]{1,0:T(8,128)S(1)} %get-tuple-element.12, f32[256,16]{1,0:T(8,128)S(1)} %get-tuple-element.11, ...), kind=kOutput, calls=%fused_computation.14 | convolution fusion | flops 35782656 | bytes 5799936 | tf_op jit(solution)/shard_map/rghp,rgpd->rghd/dot_general | solution.py:68
  156.7 5.2 %fusion = f32[256]{0:T(256)S(1)} fusion(bf16[256,16384]{1,0:T(8,128)(2,1)} %all-gather.3.cloned.1.call-done), kind=kLoop, calls=%fused_computation.3 | loop fusion | flops 12582656 | bytes 8389632 | tf_op jit(solution)/shard_map/reduce_sum | solution.py:99
  161.9 176.5 %all-gather.5.cloned.1.call-done = bf16[2,256,16384]{2,1,0:T(8,128)(2,1)} async-done(((bf16[2,8,16384]{2,1,0:T(8,128)(2,1)}), bf16[2,256,16384]{2,1,0:T(8,128)(2,1)}) %all-gather.5.cloned.1.call-update) | async-done | bytes 16777232 | tf_op jit(solution)/shard_map/all_gather | solution.py:112
  338.4 12.0 %fusion.19 = f32[256,2,32,8]{0,3,2,1:T(8,128)S(1)} fusion(bf16[2,256,16384]{2,1,0:T(8,128)(2,1)} %all-gather.5.cloned.1.call-done, bf16[256,16384]{1,0:T(8,128)(2,1)} %all-gather.3.cloned.1.call-done, f32[16384]{0:T(1024)S(1)} %copy-done.5, f32[256]{0:T(256)S(1)} %add_rsqrt_fusion), kind=kOutput, calls=%fused_computation.26 | convolution fusion | flops 4311744512 | bytes 25756672 | tf_op jit(solution)/shard_map/xk,cuk->xcu/dot_general | solution.py:109
  350.5 0.1 fusion.30
  350.5 0.6 gather_fusion
  351.1 0.1 fusion.31
  351.2 0.8 copy.23
  (22 shorter events, 0.1 us)
Async XLA Ops:
  7.2 140.7 %copy-start = (bf16[256,16,128]{2,1,0:T(8,128)(2,1)S(1)}, bf16[256,16,128]{2,1,0:T(8,128)(2,1)}, u32[]{:S(2)}) copy-start(bf16[256,16,128]{2,1,0:T(8,128)(2,1)} %param.17) | copy-start | bytes 3145732
  7.2 114.1 %copy-start.1 = (f32[2,64,2048]{2,1,0:T(8,128)S(1)}, f32[2,64,2048]{2,1,0:T(8,128)}, u32[]{:S(2)}) copy-start(f32[2,64,2048]{2,1,0:T(8,128)} %param.12) | copy-start | bytes 3145732
  7.2 149.5 %all-gather.3.cloned.1.call-start = ((), (), s32[]{:S(2)}) async-start(), calls=%async_computation.1 | async-start | bytes 9437184 | tf_op jit(solution)/shard_map/all_gather | solution.py:97
  7.9 330.5 %all-gather.5.cloned.1.call-start = ((), (), s32[]{:S(2)}) async-start(), calls=%async_computation.2 | async-start | bytes 17301504 | tf_op jit(solution)/shard_map/all_gather | solution.py:112
  125.1 22.2 %copy-start.6 = (s32[32]{0:T(128)S(1)}, s32[32]{0:T(128)}, u32[]{:S(2)}) copy-start(s32[32]{0:T(128)} %param.21) | copy-start | bytes 388
  125.1 22.4 %copy-start.3 = (bf16[256,2,1,128]{3,1,2,0:T(2,128)(2,1)S(1)}, bf16[256,2,1,128]{3,1,2,0:T(2,128)(2,1)}, u32[]{:S(2)}) copy-start(bf16[256,2,1,128]{3,1,2,0:T(2,128)(2,1)} %param.19) | copy-start | bytes 393220
  125.2 22.6 %copy-start.4 = (s32[256]{0:T(256)S(1)}, s32[256]{0:T(256)}, u32[]{:S(2)}) copy-start(s32[256]{0:T(256)} %param.20) | copy-start | bytes 3076
  148.5 4.5 %copy-start.2 = (bf16[256,2,1,32,128]{4,3,2,1,0:T(8,128)(2,1)S(1)}, bf16[256,2,1,32,128]{4,3,2,1,0:T(8,128)(2,1)}, u32[]{:S(2)}) copy-start(bf16[256,2,1,32,128]{4,3,2,1,0:T(8,128)(2,1)} %param.18) | copy-start | bytes 12582916
  156.7 181.7 %copy-start.5 = (f32[16384]{0:T(1024)S(1)}, f32[16384]{0:T(1024)}, u32[]{:S(2)}) copy-start(f32[16384]{0:T(1024)} %param.16) | copy-start | bytes 196612
Sparse Core Ops, SparseCore 0:
  9.9 90.7 all-gather.2
  147.4 190.9 all-gather.4
